TPU v7x, 256 devices: a whole 4x4x8 slice. The times are simulated.
256 devices in a mesh: dp: 32 (over y_lo, z, core), seq: 8 (over y_hi, x).
Axes of the slice: x: 4, y: 4 (y_hi: 2, y_lo: 2; y = y_hi * 2 + y_lo), z: 8, core: 2. Of those that a mesh axis runs over, the one named last changes fastest.
Arguments:
- acts: bfloat16 [32768, 4096], P(('dp', 'seq')), may hold values from -24 to 24
- grad_out: bfloat16 [32768, 4096], P('dp', 'seq'), may hold values from -6 to 6
- proj_weight: bfloat16 [4096, 4096], P('dp', 'seq'), may hold values from -0.09375 to 0.09375
Outputs:
- grad_acts: float32 [32768, 4096], P(('dp', 'seq'))
- grad_weight: float32 [4096, 4096], P('dp', 'seq')
All inputs are finite; a program needn't handle non-finite values.
Results may differ from a plain program's by a relative error of at most 0.014.
Values may be sent and summed in bfloat16 or wider, within the bound.
No kernel may reach another device: no remote copies, remote signals or barrier semaphores. Data moves between devices by JAX's collectives and lax.ppermute only.
A program may use at most 64 MiB of HBM per device.

v0:
```python
import jax
import jax.numpy as jnp
from jax import lax
from jax.sharding import Mesh, PartitionSpec as P

AXES = ("ylo", "z", "core", "yhi", "x")
SIZES = (2, 8, 2, 2, 4)
F32 = jnp.float32
BF16 = jnp.bfloat16


def from_x(value, offset):
    return lax.ppermute(value, "x", [((i + offset) % 4, i) for i in range(4)])


def swap(value, axis):
    return lax.ppermute(value, axis, [(0, 1), (1, 0)])


def rank16(ylo, core, x):
    return (ylo * 2 + core) * 4 + x


TO_BLOCK = [
    (rank16(x % 2, x // 2, (x + 2 * ylo + core) % 4), rank16(ylo, core, x))
    for ylo in range(2)
    for core in range(2)
    for x in range(4)
]
TO_OWNER = [(dst, src) for src, dst in TO_BLOCK]


def dot(a, b, contract):
    return lax.dot_general(
        a, b, ((contract[:1], contract[1:]), ((), ())), preferred_element_type=F32
    )


def per_device(acts, grad_out, weight):
    ylo, core = (lax.axis_index("ylo"), lax.axis_index("core"))
    yhi, x = (lax.axis_index("yhi"), lax.axis_index("x"))
    w = lax.ppermute(weight, ("ylo", "core", "x"), TO_BLOCK)
    w_other = swap(w, "ylo")
    w = jnp.concatenate([jnp.where(ylo == 0, w, w_other), jnp.where(ylo == 0, w_other, w)], axis=1)
    w = lax.all_gather(w, "z", axis=0, tiled=True)
    w_other = swap(w, "core")
    w_even = jnp.where(core == 0, w, w_other)
    w_odd = jnp.where(core == 0, w_other, w)
    blocks = acts.reshape(128, 2, 8, 2, 128).transpose(3, 1, 0, 2, 4).reshape(4, 128, 1024)

    def block_of(stack, k):
        return lax.dynamic_index_in_dim(stack, (x + k) % 4, 0, keepdims=False)

    half = jnp.zeros((4, 128, 1024), BF16)
    for k in range(4):
        piece = block_of(blocks, -k)
        piece = from_x(piece, k) if k else piece
        half = lax.dynamic_update_index_in_dim(half, piece, (x + k) % 4, 0)
    other = swap(half, "yhi")
    tokens = jnp.stack([jnp.where(yhi == 0, half, other), jnp.where(yhi == 0, other, half)])
    tokens = tokens.reshape(1024, 1024)
    g0 = grad_out
    g1 = from_x(g0, 1)
    g3 = from_x(g0, -1)
    g2 = jnp.concatenate([from_x(g1[:512], 1), from_x(g3[512:], -1)], axis=0)
    g = [g0, g1, g2, g3]
    terms = [dot(tokens, g_k, (0, 0)).astype(BF16) for g_k in g]
    keep = [jnp.where(core == 0, terms[0], terms[1]), jnp.where(core == 0, terms[2], terms[3])]
    give = [jnp.where(core == 0, terms[1], terms[0]), jnp.where(core == 0, terms[3], terms[2])]
    s = [(a.astype(F32) + swap(b, "core").astype(F32)).astype(BF16) for a, b in zip(keep, give)]
    keep = jnp.where(ylo == 0, s[0], s[1])
    give = jnp.where(ylo == 0, s[1], s[0])
    s = (keep.astype(F32) + swap(give, "ylo").astype(F32)).astype(BF16)
    s = lax.psum_scatter(s, "z", scatter_dimension=0, tiled=True)
    s = lax.ppermute(s, ("ylo", "core", "x"), TO_OWNER)
    grad_weight = s.astype(F32) / jnp.sqrt(F32(32768))
    part = dot(jnp.concatenate([g0, g2], axis=1), w_even, (1, 1))
    part = part + dot(jnp.concatenate([g1, g3], axis=1), w_odd, (1, 1))
    part = part.reshape(2, 512, 1024)
    give = lax.dynamic_index_in_dim(part, 1 - yhi, 0, keepdims=False).astype(BF16)
    mine = lax.dynamic_index_in_dim(part, yhi, 0, keepdims=False)
    mine = mine + swap(give, "yhi").astype(F32)
    mine = mine.reshape(4, 128, 1024)
    out = jnp.zeros((4, 128, 1024), F32)
    for k in range(4):
        piece = block_of(mine, -k)
        piece = from_x(piece.astype(BF16), k).astype(F32) if k else piece
        out = lax.dynamic_update_index_in_dim(out, piece, (x + k) % 4, 0)
    out = out.reshape(2, 2, 128, 8, 128).transpose(2, 1, 3, 0, 4).reshape(128, 4096)
    return (out, grad_weight)


def solution(mesh):
    fine = Mesh(mesh.devices.reshape(SIZES), AXES)
    rows = P(AXES, None)
    blocks = P(("ylo", "z", "core"), ("yhi", "x"))
    return jax.shard_map(
        per_device,
        mesh=fine,
        in_specs=(rows, blocks, blocks),
        out_specs=(rows, blocks),
        check_vma=False,
    )
```

profile of v0, /device:TPU:1, one launch (start us, length us, event | category | flops | bytes accessed | tf_op | source)
XLA Modules:
  0.0 232.7 jit_solution(10514562266721247765)
XLA Ops:
  10.0 3.3 %collective-permute-start.11 = (bf16[128,1024]{1,0:T(8,128)(2,1)}, bf16[128,1024]{1,0:T(8,128)(2,1)S(1)}, u32[]{:S(2)}, u32[]{:S(2)}) collective-permute-start(bf16[128,1024]{1,0:T(8,128)(2,1)} %bitcast.16), channel_id=1, source_target_pairs={{1,0},{2,1},{3,2},{0,3},{5,4},{6,5},{7,6},{4,7},{9,8},{10,9},{11,1... | collective-permute-start | bytes 786440 | tf_op jit(solution)/shard_map/ppermute | solution.py:13
  19.2 7.3 %collective-permute-start.4 = (bf16[128,512]{1,0:T(8,128)(2,1)}, bf16[128,512]{1,0:T(8,128)(2,1)S(1)}, u32[]{:S(2)}, u32[]{:S(2)}) collective-permute-start(bf16[128,512]{1,0:T(8,128)(2,1)} %param.5), channel_id=1, source_target_pairs={{0,0},{129,1},{10,2},{139,3},{1,8},{130,9},{11,10},{136,11},{2,128... | collective-permute-start | bytes 393224 | tf_op jit(solution)/shard_map/ppermute | solution.py:42
  26.5 16.3 %collective-permute-done.12 = bf16[128,1024]{1,0:T(8,128)(2,1)S(1)} collective-permute-done((bf16[128,1024]{1,0:T(8,128)(2,1)}, bf16[128,1024]{1,0:T(8,128)(2,1)S(1)}, u32[]{:S(2)}, u32[]{:S(2)}) %collective-permute-start.12) | collective-permute-done | bytes 262176 | tf_op jit(solution)/shard_map/ppermute | solution.py:13
  42.8 7.1 %collective-permute-done.13 = bf16[128,1024]{1,0:T(8,128)(2,1)S(1)} collective-permute-done((bf16[128,1024]{1,0:T(8,128)(2,1)}, bf16[128,1024]{1,0:T(8,128)(2,1)S(1)}, u32[]{:S(2)}, u32[]{:S(2)}) %collective-permute-start.13) | collective-permute-done | bytes 262176 | tf_op jit(solution)/shard_map/ppermute | solution.py:13
  49.9 3.0 %collective-permute-start.14 = (bf16[4,128,1024]{2,1,0:T(8,128)(2,1)S(1)}, bf16[4,128,1024]{2,1,0:T(8,128)(2,1)S(1)}, u32[]{:S(2)}, u32[]{:S(2)}) collective-permute-start(bf16[4,128,1024]{2,1,0:T(8,128)(2,1)S(1)} %bitcast_dynamic-update-slice_fusion), channel_id=1, source_target_pairs={{0,4},{4,0},{1,5},{5,1},{2,6},{6,2},{3,7},{7,3},{8,12},{12,8},{9,1... | collective-permute-start | bytes 3145736 | tf_op jit(solution)/shard_map/ppermute | solution.py:17
  55.4 21.8 %collective-permute-done.5 = bf16[128,512]{1,0:T(8,128)(2,1)S(1)} collective-permute-done((bf16[128,512]{1,0:T(8,128)(2,1)S(1)}, bf16[128,512]{1,0:T(8,128)(2,1)S(1)}, u32[]{:S(2)}, u32[]{:S(2)}) %collective-permute-start.5) | collective-permute-done | bytes 131104 | tf_op jit(solution)/shard_map/ppermute | solution.py:17
  83.5 2.6 %broadcast_select_fusion.1 = (bf16[1024,512]{1,0:T(8,128)(2,1)}, bf16[1024,512]{1,0:T(8,128)(2,1)}) fusion(bf16[1024,512]{1,0:T(8,128)(2,1)S(1)} %convolution_convert_fusion.3, pred[]{:T(512)S(6)} %eq.35, bf16[1024,1024]{1,0:T(8,128)(2,1)S(1)} %bitcast.60, bf16[1024,512]{1,0:T(8,128)(2,1)S(1)} %copy-done.6), kind=kOutput, calls=%fused_computation.27 | convolution fusion | flops 1074790400 | bytes 6291457 | tf_op jit(solution)/shard_map/dot_general | solution.py:34
  86.1 3.6 %collective-permute-start.15 = (bf16[1024,512]{1,0:T(8,128)(2,1)}, bf16[1024,512]{1,0:T(8,128)(2,1)S(1)}, u32[]{:S(2)}, u32[]{:S(2)}) collective-permute-start(bf16[1024,512]{1,0:T(8,128)(2,1)} %get-tuple-element.20), channel_id=1, source_target_pairs={{0,8},{8,0},{1,9},{9,1},{2,10},{10,2},{3,11},{11,3},{4,12},{12,4},... | collective-permute-start | bytes 3145736 | tf_op jit(solution)/shard_map/ppermute | solution.py:17
  92.4 4.2 %broadcast_select_fusion = (bf16[1024,512]{1,0:T(8,128)(2,1)}, bf16[1024,512]{1,0:T(8,128)(2,1)}) fusion(bf16[1024,512]{1,0:T(8,128)(2,1)S(1)} %convolution_convert_fusion.1, pred[]{:T(512)S(6)} %eq.35, bf16[1024,1024]{1,0:T(8,128)(2,1)S(1)} %bitcast.62, bf16[1024,512]{1,0:T(8,128)(2,1)} %collective-permute-done.2), kind=kOutput, calls=%fused_computation.26 | convolution fusion | flops 1074790400 | bytes 6291457 | tf_op jit(solution)/shard_map/dot_general | solution.py:34
  96.7 4.0 %collective-permute-start.16 = (bf16[1024,512]{1,0:T(8,128)(2,1)}, bf16[1024,512]{1,0:T(8,128)(2,1)S(1)}, u32[]{:S(2)}, u32[]{:S(2)}) collective-permute-start(bf16[1024,512]{1,0:T(8,128)(2,1)} %get-tuple-element.22), channel_id=1, source_target_pairs={{0,8},{8,0},{1,9},{9,1},{2,10},{10,2},{3,11},{11,3},{4,12},{12,4},... | collective-permute-start | bytes 3145736 | tf_op jit(solution)/shard_map/ppermute | solution.py:17
  100.7 16.6 %all-gather.2.cloned.1.call-done = bf16[1024,1024]{1,0:T(8,128)(2,1)} async-done(((bf16[128,1024]{1,0:T(8,128)(2,1)}), bf16[1024,1024]{1,0:T(8,128)(2,1)}) %all-gather.2.cloned.1.call-update) | async-done | bytes 2097168 | tf_op jit(solution)/shard_map/all_gather | solution.py:45
  117.3 4.6 %collective-permute-start.6 = (bf16[1024,1024]{1,0:T(8,128)(2,1)}, bf16[1024,1024]{1,0:T(8,128)(2,1)}, u32[]{:S(2)}, u32[]{:S(2)}) collective-permute-start(bf16[1024,1024]{1,0:T(8,128)(2,1)} %all-gather.2.cloned.1.call-done), channel_id=1, source_target_pairs={{0,8},{8,0},{1,9},{9,1},{2,10},{10,2},{3,11},{11,3},{4,12},{12,4},... | collective-permute-start | bytes 6291464 | tf_op jit(solution)/shard_map/ppermute | solution.py:17
  123.2 4.1 %broadcast_select_fusion.2 = (bf16[1024,512]{1,0:T(8,128)(2,1)}, bf16[1024,512]{1,0:T(8,128)(2,1)S(1)}, bf16[1024,512]{1,0:T(8,128)(2,1)S(1)}) fusion(pred[]{:T(512)S(6)} %eq.36, bf16[1024,512]{1,0:T(8,128)(2,1)} %copy-done.2, bf16[1024,512]{1,0:T(8,128)(2,1)S(1)} %convolution_convert_fusion.3, bf16[1024,512]{1,0:T(8,128)(2,1)} %get-tuple-element.21, ...), kind=kLoop, calls=%fused_computation.28 | loop fusion | flops 5767168 | bytes 9437186 | tf_op jit(solution)/shard_map/jit(_where)/select_n | solution.py:72
  128.3 24.3 %collective-permute-done.17 = bf16[1024,512]{1,0:T(8,128)(2,1)S(1)} collective-permute-done((bf16[1024,512]{1,0:T(8,128)(2,1)}, bf16[1024,512]{1,0:T(8,128)(2,1)S(1)}, u32[]{:S(2)}, u32[]{:S(2)}) %collective-permute-start.17) | collective-permute-done | bytes 1048608 | tf_op jit(solution)/shard_map/ppermute | solution.py:17
  154.0 4.8 %fusion.4 = f32[1024,1024]{1,0:T(8,128)S(1)} fusion(bf16[1024,512]{1,0:T(8,128)(2,1)} %collective-permute-done.2, bf16[1024,512]{1,0:T(8,128)(2,1)} %copy-done.5, bf16[1024,1024]{1,0:T(8,128)(2,1)} %collective-permute-done.6, bf16[1024,1024]{1,0:T(8,128)(2,1)} %all-gather.2.cloned.1.call-done, pred[]{:T(512)S(6)} %eq.35), kind=kOutput, calls=%fused_computation.4 | convolution fusion | flops 2152726528 | bytes 10485761 | tf_op jit(solution)/shard_map/dot_general | solution.py:34
  158.8 4.0 %fusion.12 = f32[1024,1024]{1,0:T(8,128)S(1)} fusion(f32[1024,1024]{1,0:T(8,128)S(1)} %fusion.4, bf16[1024,1024]{1,0:T(8,128)(2,1)S(1)} %copy-done.9, bf16[1024,1024]{1,0:T(8,128)(2,1)} %collective-permute-done.6, pred[]{:T(512)S(6)} %eq.35, bf16[1024,512]{1,0:T(8,128)(2,1)S(1)} %copy-done.8, bf16[1024,512]{1,0:T(8,128)(2,1)S(1)} %copy-done.11), kind=kOutput, calls=%fused_computation.18 | convolution fusion | flops 2153775104 | bytes 14680065 | tf_op jit(solution)/shard_map/dot_general | solution.py:34
  165.0 2.6 %collective-permute-start.7 = (bf16[512,1024]{1,0:T(8,128)(2,1)S(1)}, bf16[512,1024]{1,0:T(8,128)(2,1)S(1)}, u32[]{:S(2)}, u32[]{:S(2)}) collective-permute-start(bf16[512,1024]{1,0:T(8,128)(2,1)S(1)} %fusion.17), channel_id=1, source_target_pairs={{0,4},{4,0},{1,5},{5,1},{2,6},{6,2},{3,7},{7,3},{8,12},{12,8},{9,1... | collective-permute-start | bytes 3145736 | tf_op jit(solution)/shard_map/ppermute | solution.py:17
  167.5 19.4 %reduce-scatter.2.cloned.1.call-done = bf16[128,512]{1,0:T(8,128)(2,1)} async-done(((bf16[1024,512]{1,0:T(8,128)(2,1)}), bf16[128,512]{1,0:T(8,128)(2,1)}) %reduce-scatter.2.cloned.1.call-update) | async-done | bytes 131088 | tf_op jit(solution)/shard_map/reduce_scatter | solution.py:74
  187.0 7.6 %collective-permute-start.18 = (bf16[128,512]{1,0:T(8,128)(2,1)}, bf16[128,512]{1,0:T(8,128)(2,1)S(1)}, u32[]{:S(2)}, u32[]{:S(2)}) collective-permute-start(bf16[128,512]{1,0:T(8,128)(2,1)} %reduce-scatter.2.cloned.1.call-done), channel_id=1, source_target_pairs={{0,0},{1,129},{2,10},{3,139},{8,1},{9,130},{10,11},{11,136},{128,2... | collective-permute-start | bytes 393224 | tf_op jit(solution)/shard_map/ppermute | solution.py:75
  197.4 2.5 %collective-permute-done.18 = bf16[128,512]{1,0:T(8,128)(2,1)S(1)} collective-permute-done((bf16[128,512]{1,0:T(8,128)(2,1)}, bf16[128,512]{1,0:T(8,128)(2,1)S(1)}, u32[]{:S(2)}, u32[]{:S(2)}) %collective-permute-start.18) | collective-permute-done | bytes 131104 | tf_op jit(solution)/shard_map/ppermute | solution.py:75
  202.5 3.3 %collective-permute-done.8 = bf16[128,1024]{1,0:T(8,128)(2,1)} collective-permute-done((bf16[128,1024]{1,0:T(8,128)(2,1)S(1)}, bf16[128,1024]{1,0:T(8,128)(2,1)}, u32[]{:S(2)}, u32[]{:S(2)}) %collective-permute-start.8) | collective-permute-done | bytes 262176 | tf_op jit(solution)/shard_map/ppermute | solution.py:13
  207.0 3.0 %collective-permute-done.9 = bf16[128,1024]{1,0:T(8,128)(2,1)} collective-permute-done((bf16[128,1024]{1,0:T(8,128)(2,1)}, bf16[128,1024]{1,0:T(8,128)(2,1)}, u32[]{:S(2)}, u32[]{:S(2)}) %collective-permute-start.9) | collective-permute-done | bytes 262176 | tf_op jit(solution)/shard_map/ppermute | solution.py:13
  213.0 3.6 %collective-permute-done.10 = bf16[128,1024]{1,0:T(8,128)(2,1)} collective-permute-done((bf16[128,1024]{1,0:T(8,128)(2,1)S(1)}, bf16[128,1024]{1,0:T(8,128)(2,1)}, u32[]{:S(2)}, u32[]{:S(2)}) %collective-permute-start.10) | collective-permute-done | bytes 262176 | tf_op jit(solution)/shard_map/ppermute | solution.py:13
  223.0 2.9 %copy.25 = f32[128,4096]{1,0:T(8,128)} copy(f32[128,4096]{0,1:T(8,128)} %bitcast.52) | data formatting | bytes 4194304
  (91 shorter events, 41.6 us)
Async XLA Ops:
  7.2 110.1 %all-gather.2.cloned.1.call-start = ((), (), s32[]{:S(2)}) async-start(), calls=%async_computation.1 | async-start | bytes 2359296 | tf_op jit(solution)/shard_map/all_gather | solution.py:45
  10.0 9.2 %collective-permute-start.11 = (bf16[128,1024]{1,0:T(8,128)(2,1)}, bf16[128,1024]{1,0:T(8,128)(2,1)S(1)}, u32[]{:S(2)}, u32[]{:S(2)}) collective-permute-start(bf16[128,1024]{1,0:T(8,128)(2,1)} %bitcast.16), channel_id=1, source_target_pairs={{1,0},{2,1},{3,2},{0,3},{5,4},{6,5},{7,6},{4,7},{9,8},{10,9},{11,1... | collective-permute-start | bytes 786440 | tf_op jit(solution)/shard_map/ppermute | solution.py:13
  13.3 64.7 %collective-permute-start = (bf16[1024,512]{1,0:T(8,128)(2,1)}, bf16[1024,512]{1,0:T(8,128)(2,1)S(1)}, u32[]{:S(2)}, u32[]{:S(2)}) collective-permute-start(bf16[1024,512]{1,0:T(8,128)(2,1)} %param.4), channel_id=1, source_target_pairs={{1,0},{2,1},{3,2},{0,3},{5,4},{6,5},{7,6},{4,7},{9,8},{10,9},{11,1... | collective-permute-start | bytes 3145736 | tf_op jit(solution)/shard_map/ppermute | solution.py:13
  13.8 64.3 %collective-permute-start.2 = (bf16[1024,512]{1,0:T(8,128)(2,1)}, bf16[1024,512]{1,0:T(8,128)(2,1)}, u32[]{:S(2)}, u32[]{:S(2)}) collective-permute-start(bf16[1024,512]{1,0:T(8,128)(2,1)} %param.4), channel_id=1, source_target_pairs={{3,0},{0,1},{1,2},{2,3},{7,4},{4,5},{5,6},{6,7},{11,8},{8,9},{9,10... | collective-permute-start | bytes 3145736 | tf_op jit(solution)/shard_map/ppermute | solution.py:13
  15.6 27.2 %collective-permute-start.12 = (bf16[128,1024]{1,0:T(8,128)(2,1)}, bf16[128,1024]{1,0:T(8,128)(2,1)S(1)}, u32[]{:S(2)}, u32[]{:S(2)}) collective-permute-start(bf16[128,1024]{1,0:T(8,128)(2,1)} %bitcast.18), channel_id=1, source_target_pairs={{2,0},{3,1},{0,2},{1,3},{6,4},{7,5},{4,6},{5,7},{10,8},{11,9},{8,1... | collective-permute-start | bytes 786440 | tf_op jit(solution)/shard_map/ppermute | solution.py:13
  17.0 32.9 %collective-permute-start.13 = (bf16[128,1024]{1,0:T(8,128)(2,1)}, bf16[128,1024]{1,0:T(8,128)(2,1)S(1)}, u32[]{:S(2)}, u32[]{:S(2)}) collective-permute-start(bf16[128,1024]{1,0:T(8,128)(2,1)} %bitcast.20), channel_id=1, source_target_pairs={{3,0},{0,1},{1,2},{2,3},{7,4},{4,5},{5,6},{6,7},{11,8},{8,9},{9,10... | collective-permute-start | bytes 786440 | tf_op jit(solution)/shard_map/ppermute | solution.py:13
  19.2 33.8 %collective-permute-start.4 = (bf16[128,512]{1,0:T(8,128)(2,1)}, bf16[128,512]{1,0:T(8,128)(2,1)S(1)}, u32[]{:S(2)}, u32[]{:S(2)}) collective-permute-start(bf16[128,512]{1,0:T(8,128)(2,1)} %param.5), channel_id=1, source_target_pairs={{0,0},{129,1},{10,2},{139,3},{1,8},{130,9},{11,10},{136,11},{2,128... | collective-permute-start | bytes 393224 | tf_op jit(solution)/shard_map/ppermute | solution.py:42
  49.9 30.8 %collective-permute-start.14 = (bf16[4,128,1024]{2,1,0:T(8,128)(2,1)S(1)}, bf16[4,128,1024]{2,1,0:T(8,128)(2,1)S(1)}, u32[]{:S(2)}, u32[]{:S(2)}) collective-permute-start(bf16[4,128,1024]{2,1,0:T(8,128)(2,1)S(1)} %bitcast_dynamic-update-slice_fusion), channel_id=1, source_target_pairs={{0,4},{4,0},{1,5},{5,1},{2,6},{6,2},{3,7},{7,3},{8,12},{12,8},{9,1... | collective-permute-start | bytes 3145736 | tf_op jit(solution)/shard_map/ppermute | solution.py:17
  52.9 24.2 %collective-permute-start.5 = (bf16[128,512]{1,0:T(8,128)(2,1)S(1)}, bf16[128,512]{1,0:T(8,128)(2,1)S(1)}, u32[]{:S(2)}, u32[]{:S(2)}) collective-permute-start(bf16[128,512]{1,0:T(8,128)(2,1)S(1)} %collective-permute-done.4), channel_id=1, source_target_pairs={{0,128},{128,0},{1,129},{129,1},{2,130},{130,2},{3,131},{131,3},{4... | collective-permute-start | bytes 393224 | tf_op jit(solution)/shard_map/ppermute | solution.py:17
  77.9 109.0 %reduce-scatter.2.cloned.1.call-start = ((), (), s32[]{:S(2)}) async-start(), calls=%async_computation.2 | async-start | bytes 1179648 | tf_op jit(solution)/shard_map/reduce_scatter | solution.py:74
  78.1 11.7 %collective-permute-start.1 = (bf16[512,512]{1,0:T(8,128)(2,1)S(1)}, bf16[512,512]{1,0:T(8,128)(2,1)S(1)}, u32[]{:S(2)}, u32[]{:S(2)}) collective-permute-start(bf16[512,512]{1,0:T(8,128)(2,1)S(1)} %slice.8), channel_id=1, source_target_pairs={{1,0},{2,1},{3,2},{0,3},{5,4},{6,5},{7,6},{4,7},{9,8},{10,9},{11,1... | collective-permute-start | bytes 1572872 | tf_op jit(solution)/shard_map/ppermute | solution.py:13
  79.5 11.6 %collective-permute-start.3 = (bf16[512,512]{1,0:T(8,128)(2,1)S(1)}, bf16[512,512]{1,0:T(8,128)(2,1)S(1)}, u32[]{:S(2)}, u32[]{:S(2)}) collective-permute-start(bf16[512,512]{1,0:T(8,128)(2,1)S(1)} %slice.9), channel_id=1, source_target_pairs={{3,0},{0,1},{1,2},{2,3},{7,4},{4,5},{5,6},{6,7},{11,8},{8,9},{9,10... | collective-permute-start | bytes 1572872 | tf_op jit(solution)/shard_map/ppermute | solution.py:13
  86.1 35.8 %collective-permute-start.15 = (bf16[1024,512]{1,0:T(8,128)(2,1)}, bf16[1024,512]{1,0:T(8,128)(2,1)S(1)}, u32[]{:S(2)}, u32[]{:S(2)}) collective-permute-start(bf16[1024,512]{1,0:T(8,128)(2,1)} %get-tuple-element.20), channel_id=1, source_target_pairs={{0,8},{8,0},{1,9},{9,1},{2,10},{10,2},{3,11},{11,3},{4,12},{12,4},... | collective-permute-start | bytes 3145736 | tf_op jit(solution)/shard_map/ppermute | solution.py:17
  96.7 25.2 %collective-permute-start.16 = (bf16[1024,512]{1,0:T(8,128)(2,1)}, bf16[1024,512]{1,0:T(8,128)(2,1)S(1)}, u32[]{:S(2)}, u32[]{:S(2)}) collective-permute-start(bf16[1024,512]{1,0:T(8,128)(2,1)} %get-tuple-element.22), channel_id=1, source_target_pairs={{0,8},{8,0},{1,9},{9,1},{2,10},{10,2},{3,11},{11,3},{4,12},{12,4},... | collective-permute-start | bytes 3145736 | tf_op jit(solution)/shard_map/ppermute | solution.py:17
  117.3 36.7 %collective-permute-start.6 = (bf16[1024,1024]{1,0:T(8,128)(2,1)}, bf16[1024,1024]{1,0:T(8,128)(2,1)}, u32[]{:S(2)}, u32[]{:S(2)}) collective-permute-start(bf16[1024,1024]{1,0:T(8,128)(2,1)} %all-gather.2.cloned.1.call-done), channel_id=1, source_target_pairs={{0,8},{8,0},{1,9},{9,1},{2,10},{10,2},{3,11},{11,3},{4,12},{12,4},... | collective-permute-start | bytes 6291464 | tf_op jit(solution)/shard_map/ppermute | solution.py:17
  127.3 25.2 %collective-permute-start.17 = (bf16[1024,512]{1,0:T(8,128)(2,1)}, bf16[1024,512]{1,0:T(8,128)(2,1)S(1)}, u32[]{:S(2)}, u32[]{:S(2)}) collective-permute-start(bf16[1024,512]{1,0:T(8,128)(2,1)} %get-tuple-element.6), channel_id=1, source_target_pairs={{0,128},{128,0},{1,129},{129,1},{2,130},{130,2},{3,131},{131,3},{4... | collective-permute-start | bytes 3145736 | tf_op jit(solution)/shard_map/ppermute | solution.py:17
  154.0 4.8 %copy-start.8 = (bf16[1024,512]{1,0:T(8,128)(2,1)S(1)}, bf16[1024,512]{1,0:T(8,128)(2,1)}, u32[]{:S(2)}) copy-start(bf16[1024,512]{1,0:T(8,128)(2,1)} %copy-done.7) | copy-start | bytes 3145732
  154.0 4.8 %copy-start.9 = (bf16[1024,1024]{1,0:T(8,128)(2,1)S(1)}, bf16[1024,1024]{1,0:T(8,128)(2,1)}, u32[]{:S(2)}) copy-start(bf16[1024,1024]{1,0:T(8,128)(2,1)} %all-gather.2.cloned.1.call-done) | copy-start | bytes 6291460
  154.0 4.8 %copy-start.11 = (bf16[1024,512]{1,0:T(8,128)(2,1)S(1)}, bf16[1024,512]{1,0:T(8,128)(2,1)}, u32[]{:S(2)}) copy-start(bf16[1024,512]{1,0:T(8,128)(2,1)} %param.4) | copy-start | bytes 3145732
  165.0 29.7 %collective-permute-start.7 = (bf16[512,1024]{1,0:T(8,128)(2,1)S(1)}, bf16[512,1024]{1,0:T(8,128)(2,1)S(1)}, u32[]{:S(2)}, u32[]{:S(2)}) collective-permute-start(bf16[512,1024]{1,0:T(8,128)(2,1)S(1)} %fusion.17), channel_id=1, source_target_pairs={{0,4},{4,0},{1,5},{5,1},{2,6},{6,2},{3,7},{7,3},{8,12},{12,8},{9,1... | collective-permute-start | bytes 3145736 | tf_op jit(solution)/shard_map/ppermute | solution.py:17
  187.0 12.9 %collective-permute-start.18 = (bf16[128,512]{1,0:T(8,128)(2,1)}, bf16[128,512]{1,0:T(8,128)(2,1)S(1)}, u32[]{:S(2)}, u32[]{:S(2)}) collective-permute-start(bf16[128,512]{1,0:T(8,128)(2,1)} %reduce-scatter.2.cloned.1.call-done), channel_id=1, source_target_pairs={{0,0},{1,129},{2,10},{3,139},{8,1},{9,130},{10,11},{11,136},{128,2... | collective-permute-start | bytes 393224 | tf_op jit(solution)/shard_map/ppermute | solution.py:75
  197.4 8.4 %collective-permute-start.8 = (bf16[128,1024]{1,0:T(8,128)(2,1)S(1)}, bf16[128,1024]{1,0:T(8,128)(2,1)}, u32[]{:S(2)}, u32[]{:S(2)}) collective-permute-start(bf16[128,1024]{1,0:T(8,128)(2,1)S(1)} %get-tuple-element.13), channel_id=1, source_target_pairs={{1,0},{2,1},{3,2},{0,3},{5,4},{6,5},{7,6},{4,7},{9,8},{10,9},{11,1... | collective-permute-start | bytes 786440 | tf_op jit(solution)/shard_map/ppermute | solution.py:13
  200.8 9.1 %collective-permute-start.9 = (bf16[128,1024]{1,0:T(8,128)(2,1)}, bf16[128,1024]{1,0:T(8,128)(2,1)}, u32[]{:S(2)}, u32[]{:S(2)}) collective-permute-start(bf16[128,1024]{1,0:T(8,128)(2,1)} %get-tuple-element.12), channel_id=1, source_target_pairs={{2,0},{3,1},{0,2},{1,3},{6,4},{7,5},{4,6},{5,7},{10,8},{11,9},{8,1... | collective-permute-start | bytes 786440 | tf_op jit(solution)/shard_map/ppermute | solution.py:13
  202.3 14.3 %collective-permute-start.10 = (bf16[128,1024]{1,0:T(8,128)(2,1)S(1)}, bf16[128,1024]{1,0:T(8,128)(2,1)}, u32[]{:S(2)}, u32[]{:S(2)}) collective-permute-start(bf16[128,1024]{1,0:T(8,128)(2,1)S(1)} %get-tuple-element.11), channel_id=1, source_target_pairs={{3,0},{0,1},{1,2},{2,3},{7,4},{4,5},{5,6},{6,7},{11,8},{8,9},{9,10... | collective-permute-start | bytes 786440 | tf_op jit(solution)/shard_map/ppermute | solution.py:13
  (9 other events, 16.3 us)
Sparse Core Ops, SparseCore 0:
  78.1 39.1 all-gather.1
  154.1 32.8 reduce-scatter.1
where the time goes:
time: 233 us
  waiting for transfers between devices  119 us (51%)
  starting transfers between devices  46.2 us (20%)
  local copies, waits for them, and re-layouts  20.7 us (9%)
  matrix products  18.2 us (8%)
  between operations  14.6 us (6%)
  other arithmetic  13.8 us (6%)
    ppermute x7, waiting for transfers between devices, swap(): return lax.ppermute(value, axis, [(0, 1), (1, 0)])  46.1 us
    ppermute x10, waiting for transfers between devices, from_x(): return lax.ppermute(value, 'x', [((i + offset) % 4, i) for i in range(4)])  34.6 us
    ppermute x7, starting transfers between devices, swap(): return lax.ppermute(value, axis, [(0, 1), (1, 0)])  21.3 us
    reduce_scatter x1, waiting for transfers between devices, per_device(): s = lax.psum_scatter(s, 'z', scatter_dimension=0, tiled=True)  19.4 us
    dot_general x6, matrix products, dot(): lax.dot_general(a, b, ((contract[:1], contract[1:]), ((), ())), preferred...  18.2 us
    all_gather x1, waiting for transfers between devices, per_device(): w = lax.all_gather(w, 'z', axis=0, tiled=True)  16.6 us
    ppermute x10, starting transfers between devices, from_x(): return lax.ppermute(value, 'x', [((i + offset) % 4, i) for i in range(4)])  9.94 us
    unnamed x27, local copies, waits for them, and re-layouts  9.8 us
  transfers between devices with their start and end apart: 21, of which 11 were waited for; matrix products, arithmetic and copies ran while one was open for 16% of the time, Pallas kernels for 0%

commit v1 on v0

--- a/solution.py
+++ b/solution.py
@@ -42,7 +42,15 @@
     w = lax.ppermute(weight, ("ylo", "core", "x"), TO_BLOCK)
     w_other = swap(w, "ylo")
     w = jnp.concatenate([jnp.where(ylo == 0, w, w_other), jnp.where(ylo == 0, w_other, w)], axis=1)
-    w = lax.all_gather(w, "z", axis=0, tiled=True)
+    w = jnp.concatenate(
+        jax.lax.all_to_all(
+            jnp.stack([w for _ in range(jax.lax.axis_size("z"))]),
+            axis_name="z",
+            split_axis=0,
+            concat_axis=0,
+        ),
+        axis=0,
+    )
     w_other = swap(w, "core")
     w_even = jnp.where(core == 0, w, w_other)
     w_odd = jnp.where(core == 0, w_other, w)

time: 233 us -> 245 us (1.052)
  starting transfers between devices: 46.2 us -> 52.1 us
  waiting for transfers between devices: 119 us -> 124 us
    all_to_all x0 -> x1, waiting for transfers between devices: none -> 26 us  [per_device(): jax.lax.all_to_all(jnp.stack([w for _ in range(jax.lax.axis_size('z'))]),...]
    all_gather x1 -> x0, waiting for transfers between devices: 16.6 us -> none  [per_device(): w = lax.all_gather(w, 'z', axis=0, tiled=True)]
    all_to_all x0 -> x1, starting transfers between devices: none -> 8.19 us  [per_device(): jax.lax.all_to_all(jnp.stack([w for _ in range(jax.lax.axis_size('z'))]),...]
    reduce_scatter x1, waiting for transfers between devices: 19.4 us -> 14.8 us  [per_device(): s = lax.psum_scatter(s, 'z', scatter_dimension=0, tiled=True)]
    unnamed x27 -> x25, local copies, waits for them, and re-layouts: 9.8 us -> 9.83 us
  transfers between devices with their start and end apart: 21 -> 21, of which waited for: 11 -> 12; matrix products, arithmetic and copies ran while one was open for 16% -> 15% of each run, Pallas kernels for 0% -> 0%
where the time goes in v1:
time: 245 us; the launch traced here: 244 us
  waiting for transfers between devices  124 us (51%)
  starting transfers between devices  52.1 us (21%)
  local copies, waits for them, and re-layouts  22.3 us (9%)
  matrix products  18.3 us (7%)
  between operations  14.6 us (6%)
  other arithmetic  13 us (5%)
    ppermute x7, waiting for transfers between devices, swap(): return lax.ppermute(value, axis, [(0, 1), (1, 0)])  48.4 us
    ppermute x10, waiting for transfers between devices, from_x(): return lax.ppermute(value, 'x', [((i + offset) % 4, i) for i in range(4)])  33.8 us
    all_to_all x1, waiting for transfers between devices, per_device(): jax.lax.all_to_all(jnp.stack([w for _ in range(jax.lax.axis_size('z'))]),...  26 us
    ppermute x7, starting transfers between devices, swap(): return lax.ppermute(value, axis, [(0, 1), (1, 0)])  18.9 us
    dot_general x6, matrix products, dot(): lax.dot_general(a, b, ((contract[:1], contract[1:]), ((), ())), preferred...  18.3 us
    reduce_scatter x1, waiting for transfers between devices, per_device(): s = lax.psum_scatter(s, 'z', scatter_dimension=0, tiled=True)  14.8 us
    ppermute x10, starting transfers between devices, from_x(): return lax.ppermute(value, 'x', [((i + offset) % 4, i) for i in range(4)])  9.94 us
    unnamed x25, local copies, waits for them, and re-layouts  9.83 us
  transfers between devices with their start and end apart: 21, of which 12 were waited for; matrix products, arithmetic and copies ran while one was open for 15% of the time, Pallas kernels for 0%

profile of v1, /device:TPU:1, one launch (start us, length us, event | category | flops | bytes accessed | tf_op | source)
XLA Modules:
  0.0 244.5 jit_solution(10187919375621214478)
XLA Ops:
  9.9 3.3 %collective-permute-start.11 = (bf16[128,1024]{1,0:T(8,128)(2,1)}, bf16[128,1024]{1,0:T(8,128)(2,1)S(1)}, u32[]{:S(2)}, u32[]{:S(2)}) collective-permute-start(bf16[128,1024]{1,0:T(8,128)(2,1)} %bitcast.17), channel_id=1, source_target_pairs={{1,0},{2,1},{3,2},{0,3},{5,4},{6,5},{7,6},{4,7},{9,8},{10,9},{11,1... | collective-permute-start | bytes 786440 | tf_op jit(solution)/shard_map/ppermute | solution.py:13
  19.1 7.3 %collective-permute-start.4 = (bf16[128,512]{1,0:T(8,128)(2,1)}, bf16[128,512]{1,0:T(8,128)(2,1)S(1)}, u32[]{:S(2)}, u32[]{:S(2)}) collective-permute-start(bf16[128,512]{1,0:T(8,128)(2,1)} %param.5), channel_id=1, source_target_pairs={{0,0},{129,1},{10,2},{139,3},{1,8},{130,9},{11,10},{136,11},{2,128... | collective-permute-start | bytes 393224 | tf_op jit(solution)/shard_map/ppermute | solution.py:42
  26.4 16.3 %collective-permute-done.12 = bf16[128,1024]{1,0:T(8,128)(2,1)S(1)} collective-permute-done((bf16[128,1024]{1,0:T(8,128)(2,1)}, bf16[128,1024]{1,0:T(8,128)(2,1)S(1)}, u32[]{:S(2)}, u32[]{:S(2)}) %collective-permute-start.12) | collective-permute-done | bytes 262176 | tf_op jit(solution)/shard_map/ppermute | solution.py:13
  42.8 7.1 %collective-permute-done.13 = bf16[128,1024]{1,0:T(8,128)(2,1)S(1)} collective-permute-done((bf16[128,1024]{1,0:T(8,128)(2,1)}, bf16[128,1024]{1,0:T(8,128)(2,1)S(1)}, u32[]{:S(2)}, u32[]{:S(2)}) %collective-permute-start.13) | collective-permute-done | bytes 262176 | tf_op jit(solution)/shard_map/ppermute | solution.py:13
  49.9 3.0 %collective-permute-start.14 = (bf16[4,128,1024]{2,1,0:T(8,128)(2,1)S(1)}, bf16[4,128,1024]{2,1,0:T(8,128)(2,1)S(1)}, u32[]{:S(2)}, u32[]{:S(2)}) collective-permute-start(bf16[4,128,1024]{2,1,0:T(8,128)(2,1)S(1)} %bitcast_dynamic-update-slice_fusion), channel_id=1, source_target_pairs={{0,4},{4,0},{1,5},{5,1},{2,6},{6,2},{3,7},{7,3},{8,12},{12,8},{9,1... | collective-permute-start | bytes 3145736 | tf_op jit(solution)/shard_map/ppermute | solution.py:17
  52.9 2.4 collective-permute-start.5
  55.3 21.8 %collective-permute-done.5 = bf16[128,512]{1,0:T(8,128)(2,1)S(1)} collective-permute-done((bf16[128,512]{1,0:T(8,128)(2,1)S(1)}, bf16[128,512]{1,0:T(8,128)(2,1)S(1)}, u32[]{:S(2)}, u32[]{:S(2)}) %collective-permute-start.5) | collective-permute-done | bytes 131104 | tf_op jit(solution)/shard_map/ppermute | solution.py:17
  78.8 8.2 %all-to-all-start = ((bf16[8,128,1024]{2,1,0:T(8,128)(2,1)}), bf16[8,128,1024]{2,1,0:T(8,128)(2,1)}, u32[]{:S(2)}, u32[]{:S(2)}) async-start(bf16[8,128,1024]{2,1,0:T(8,128)(2,1)} %stack.8), calls=%async_computation | async-start | bytes 4194304 | tf_op jit(solution)/shard_map/all_to_all | solution.py:46
  92.4 2.7 %broadcast_select_fusion.1 = (bf16[1024,512]{1,0:T(8,128)(2,1)}, bf16[1024,512]{1,0:T(8,128)(2,1)}) fusion(bf16[1024,512]{1,0:T(8,128)(2,1)S(1)} %convolution_convert_fusion.3, pred[]{:T(512)S(6)} %eq.35, bf16[1024,1024]{1,0:T(8,128)(2,1)S(1)} %bitcast.61, bf16[1024,512]{1,0:T(8,128)(2,1)S(1)} %copy-done.6), kind=kOutput, calls=%fused_computation.27 | convolution fusion | flops 1074790400 | bytes 6291457 | tf_op jit(solution)/shard_map/dot_general | solution.py:34
  95.1 3.9 %collective-permute-start.15 = (bf16[1024,512]{1,0:T(8,128)(2,1)}, bf16[1024,512]{1,0:T(8,128)(2,1)S(1)}, u32[]{:S(2)}, u32[]{:S(2)}) collective-permute-start(bf16[1024,512]{1,0:T(8,128)(2,1)} %get-tuple-element.20), channel_id=1, source_target_pairs={{0,8},{8,0},{1,9},{9,1},{2,10},{10,2},{3,11},{11,3},{4,12},{12,4},... | collective-permute-start | bytes 3145736 | tf_op jit(solution)/shard_map/ppermute | solution.py:17
  101.3 4.3 %broadcast_select_fusion = (bf16[1024,512]{1,0:T(8,128)(2,1)}, bf16[1024,512]{1,0:T(8,128)(2,1)}) fusion(bf16[1024,512]{1,0:T(8,128)(2,1)S(1)} %convolution_convert_fusion.1, pred[]{:T(512)S(6)} %eq.35, bf16[1024,1024]{1,0:T(8,128)(2,1)S(1)} %bitcast.63, bf16[1024,512]{1,0:T(8,128)(2,1)} %collective-permute-done.2), kind=kOutput, calls=%fused_computation.26 | convolution fusion | flops 1074790400 | bytes 6291457 | tf_op jit(solution)/shard_map/dot_general | solution.py:34
  105.5 4.2 %collective-permute-start.16 = (bf16[1024,512]{1,0:T(8,128)(2,1)}, bf16[1024,512]{1,0:T(8,128)(2,1)S(1)}, u32[]{:S(2)}, u32[]{:S(2)}) collective-permute-start(bf16[1024,512]{1,0:T(8,128)(2,1)} %get-tuple-element.22), channel_id=1, source_target_pairs={{0,8},{8,0},{1,9},{9,1},{2,10},{10,2},{3,11},{11,3},{4,12},{12,4},... | collective-permute-start | bytes 3145736 | tf_op jit(solution)/shard_map/ppermute | solution.py:17
  109.7 26.0 %all-to-all-done = bf16[8,128,1024]{2,1,0:T(8,128)(2,1)} async-done(((bf16[8,128,1024]{2,1,0:T(8,128)(2,1)}), bf16[8,128,1024]{2,1,0:T(8,128)(2,1)}, u32[]{:S(2)}, u32[]{:S(2)}) %all-to-all-start) | async-done | bytes 2097184 | tf_op jit(solution)/shard_map/all_to_all | solution.py:46
  135.7 3.5 %collective-permute-start.6 = (bf16[1024,1024]{1,0:T(8,128)(2,1)}, bf16[1024,1024]{1,0:T(8,128)(2,1)}, u32[]{:S(2)}, u32[]{:S(2)}) collective-permute-start(bf16[1024,1024]{1,0:T(8,128)(2,1)} %bitcast), channel_id=1, source_target_pairs={{0,8},{8,0},{1,9},{9,1},{2,10},{10,2},{3,11},{11,3},{4,12},{12,4},... | collective-permute-start | bytes 6291464 | tf_op jit(solution)/shard_map/ppermute | solution.py:17
  140.6 4.0 %broadcast_select_fusion.2 = (bf16[1024,512]{1,0:T(8,128)(2,1)}, bf16[1024,512]{1,0:T(8,128)(2,1)S(1)}, bf16[1024,512]{1,0:T(8,128)(2,1)S(1)}) fusion(pred[]{:T(512)S(6)} %eq.36, bf16[1024,512]{1,0:T(8,128)(2,1)} %copy-done.2, bf16[1024,512]{1,0:T(8,128)(2,1)S(1)} %convolution_convert_fusion.3, bf16[1024,512]{1,0:T(8,128)(2,1)} %get-tuple-element.21, ...), kind=kLoop, calls=%fused_computation.28 | loop fusion | flops 5767168 | bytes 9437186 | tf_op jit(solution)/shard_map/jit(_where)/select_n | solution.py:80
  144.6 25.2 %collective-permute-done.17 = bf16[1024,512]{1,0:T(8,128)(2,1)S(1)} collective-permute-done((bf16[1024,512]{1,0:T(8,128)(2,1)}, bf16[1024,512]{1,0:T(8,128)(2,1)S(1)}, u32[]{:S(2)}, u32[]{:S(2)}) %collective-permute-start.17) | collective-permute-done | bytes 1048608 | tf_op jit(solution)/shard_map/ppermute | solution.py:17
  171.3 4.7 %fusion.4 = f32[1024,1024]{1,0:T(8,128)S(1)} fusion(bf16[1024,512]{1,0:T(8,128)(2,1)} %collective-permute-done.2, bf16[1024,512]{1,0:T(8,128)(2,1)} %copy-done.5, bf16[1024,1024]{1,0:T(8,128)(2,1)} %collective-permute-done.6, bf16[1024,1024]{1,0:T(8,128)(2,1)} %bitcast, pred[]{:T(512)S(6)} %eq.35), kind=kOutput, calls=%fused_computation.4 | convolution fusion | flops 2152726528 | bytes 10485761 | tf_op jit(solution)/shard_map/dot_general | solution.py:34
  176.0 4.1 %fusion.12 = f32[1024,1024]{1,0:T(8,128)S(1)} fusion(f32[1024,1024]{1,0:T(8,128)S(1)} %fusion.4, bf16[1024,1024]{1,0:T(8,128)(2,1)} %bitcast, bf16[1024,1024]{1,0:T(8,128)(2,1)} %collective-permute-done.6, pred[]{:T(512)S(6)} %eq.35, bf16[1024,512]{1,0:T(8,128)(2,1)S(1)} %copy-done.8, bf16[1024,512]{1,0:T(8,128)(2,1)S(1)} %copy-done.10), kind=kOutput, calls=%fused_computation.18 | convolution fusion | flops 2153775104 | bytes 14680065 | tf_op jit(solution)/shard_map/dot_general | solution.py:34
  184.2 14.8 %reduce-scatter.2.cloned.1.call-done = bf16[128,512]{1,0:T(8,128)(2,1)} async-done(((bf16[1024,512]{1,0:T(8,128)(2,1)}), bf16[128,512]{1,0:T(8,128)(2,1)}) %reduce-scatter.2.cloned.1.call-update) | async-done | bytes 131088 | tf_op jit(solution)/shard_map/reduce_scatter | solution.py:82
  198.9 7.8 %collective-permute-start.18 = (bf16[128,512]{1,0:T(8,128)(2,1)}, bf16[128,512]{1,0:T(8,128)(2,1)S(1)}, u32[]{:S(2)}, u32[]{:S(2)}) collective-permute-start(bf16[128,512]{1,0:T(8,128)(2,1)} %reduce-scatter.2.cloned.1.call-done), channel_id=1, source_target_pairs={{0,0},{1,129},{2,10},{3,139},{8,1},{9,130},{10,11},{11,136},{128,2... | collective-permute-start | bytes 393224 | tf_op jit(solution)/shard_map/ppermute | solution.py:83
  217.3 3.8 %collective-permute-done.9 = bf16[128,1024]{1,0:T(8,128)(2,1)} collective-permute-done((bf16[128,1024]{1,0:T(8,128)(2,1)}, bf16[128,1024]{1,0:T(8,128)(2,1)}, u32[]{:S(2)}, u32[]{:S(2)}) %collective-permute-start.9) | collective-permute-done | bytes 262176 | tf_op jit(solution)/shard_map/ppermute | solution.py:13
  224.1 4.2 %collective-permute-done.10 = bf16[128,1024]{1,0:T(8,128)(2,1)} collective-permute-done((bf16[128,1024]{1,0:T(8,128)(2,1)S(1)}, bf16[128,1024]{1,0:T(8,128)(2,1)}, u32[]{:S(2)}, u32[]{:S(2)}) %collective-permute-start.10) | collective-permute-done | bytes 262176 | tf_op jit(solution)/shard_map/ppermute | solution.py:13
  230.2 2.0 copy.17
  234.8 2.9 %copy.25 = f32[128,4096]{1,0:T(8,128)} copy(f32[128,4096]{0,1:T(8,128)} %bitcast.53) | data formatting | bytes 4194304
  (89 shorter events, 42.4 us)
Async XLA Ops:
  9.9 9.2 %collective-permute-start.11 = (bf16[128,1024]{1,0:T(8,128)(2,1)}, bf16[128,1024]{1,0:T(8,128)(2,1)S(1)}, u32[]{:S(2)}, u32[]{:S(2)}) collective-permute-start(bf16[128,1024]{1,0:T(8,128)(2,1)} %bitcast.17), channel_id=1, source_target_pairs={{1,0},{2,1},{3,2},{0,3},{5,4},{6,5},{7,6},{4,7},{9,8},{10,9},{11,1... | collective-permute-start | bytes 786440 | tf_op jit(solution)/shard_map/ppermute | solution.py:13
  13.2 73.8 %collective-permute-start = (bf16[1024,512]{1,0:T(8,128)(2,1)}, bf16[1024,512]{1,0:T(8,128)(2,1)S(1)}, u32[]{:S(2)}, u32[]{:S(2)}) collective-permute-start(bf16[1024,512]{1,0:T(8,128)(2,1)} %param.4), channel_id=1, source_target_pairs={{1,0},{2,1},{3,2},{0,3},{5,4},{6,5},{7,6},{4,7},{9,8},{10,9},{11,1... | collective-permute-start | bytes 3145736 | tf_op jit(solution)/shard_map/ppermute | solution.py:13
  13.8 73.4 %collective-permute-start.2 = (bf16[1024,512]{1,0:T(8,128)(2,1)}, bf16[1024,512]{1,0:T(8,128)(2,1)}, u32[]{:S(2)}, u32[]{:S(2)}) collective-permute-start(bf16[1024,512]{1,0:T(8,128)(2,1)} %param.4), channel_id=1, source_target_pairs={{3,0},{0,1},{1,2},{2,3},{7,4},{4,5},{5,6},{6,7},{11,8},{8,9},{9,10... | collective-permute-start | bytes 3145736 | tf_op jit(solution)/shard_map/ppermute | solution.py:13
  15.6 27.2 %collective-permute-start.12 = (bf16[128,1024]{1,0:T(8,128)(2,1)}, bf16[128,1024]{1,0:T(8,128)(2,1)S(1)}, u32[]{:S(2)}, u32[]{:S(2)}) collective-permute-start(bf16[128,1024]{1,0:T(8,128)(2,1)} %bitcast.19), channel_id=1, source_target_pairs={{2,0},{3,1},{0,2},{1,3},{6,4},{7,5},{4,6},{5,7},{10,8},{11,9},{8,1... | collective-permute-start | bytes 786440 | tf_op jit(solution)/shard_map/ppermute | solution.py:13
  16.9 32.9 %collective-permute-start.13 = (bf16[128,1024]{1,0:T(8,128)(2,1)}, bf16[128,1024]{1,0:T(8,128)(2,1)S(1)}, u32[]{:S(2)}, u32[]{:S(2)}) collective-permute-start(bf16[128,1024]{1,0:T(8,128)(2,1)} %bitcast.21), channel_id=1, source_target_pairs={{3,0},{0,1},{1,2},{2,3},{7,4},{4,5},{5,6},{6,7},{11,8},{8,9},{9,10... | collective-permute-start | bytes 786440 | tf_op jit(solution)/shard_map/ppermute | solution.py:13
  19.1 33.8 %collective-permute-start.4 = (bf16[128,512]{1,0:T(8,128)(2,1)}, bf16[128,512]{1,0:T(8,128)(2,1)S(1)}, u32[]{:S(2)}, u32[]{:S(2)}) collective-permute-start(bf16[128,512]{1,0:T(8,128)(2,1)} %param.5), channel_id=1, source_target_pairs={{0,0},{129,1},{10,2},{139,3},{1,8},{130,9},{11,10},{136,11},{2,128... | collective-permute-start | bytes 393224 | tf_op jit(solution)/shard_map/ppermute | solution.py:42
  49.9 39.9 %collective-permute-start.14 = (bf16[4,128,1024]{2,1,0:T(8,128)(2,1)S(1)}, bf16[4,128,1024]{2,1,0:T(8,128)(2,1)S(1)}, u32[]{:S(2)}, u32[]{:S(2)}) collective-permute-start(bf16[4,128,1024]{2,1,0:T(8,128)(2,1)S(1)} %bitcast_dynamic-update-slice_fusion), channel_id=1, source_target_pairs={{0,4},{4,0},{1,5},{5,1},{2,6},{6,2},{3,7},{7,3},{8,12},{12,8},{9,1... | collective-permute-start | bytes 3145736 | tf_op jit(solution)/shard_map/ppermute | solution.py:17
  52.9 24.2 %collective-permute-start.5 = (bf16[128,512]{1,0:T(8,128)(2,1)S(1)}, bf16[128,512]{1,0:T(8,128)(2,1)S(1)}, u32[]{:S(2)}, u32[]{:S(2)}) collective-permute-start(bf16[128,512]{1,0:T(8,128)(2,1)S(1)} %collective-permute-done.4), channel_id=1, source_target_pairs={{0,128},{128,0},{1,129},{129,1},{2,130},{130,2},{3,131},{131,3},{4... | collective-permute-start | bytes 393224 | tf_op jit(solution)/shard_map/ppermute | solution.py:17
  78.8 57.0 %all-to-all-start = ((bf16[8,128,1024]{2,1,0:T(8,128)(2,1)}), bf16[8,128,1024]{2,1,0:T(8,128)(2,1)}, u32[]{:S(2)}, u32[]{:S(2)}) async-start(bf16[8,128,1024]{2,1,0:T(8,128)(2,1)} %stack.8), calls=%async_computation | async-start | bytes 4194304 | tf_op jit(solution)/shard_map/all_to_all | solution.py:46
  86.9 112.0 %reduce-scatter.2.cloned.1.call-start = ((), (), s32[]{:S(2)}) async-start(), calls=%async_computation.2 | async-start | bytes 1179648 | tf_op jit(solution)/shard_map/reduce_scatter | solution.py:82
  87.1 12.0 %collective-permute-start.1 = (bf16[512,512]{1,0:T(8,128)(2,1)S(1)}, bf16[512,512]{1,0:T(8,128)(2,1)S(1)}, u32[]{:S(2)}, u32[]{:S(2)}) collective-permute-start(bf16[512,512]{1,0:T(8,128)(2,1)S(1)} %slice.8), channel_id=1, source_target_pairs={{1,0},{2,1},{3,2},{0,3},{5,4},{6,5},{7,6},{4,7},{9,8},{10,9},{11,1... | collective-permute-start | bytes 1572872 | tf_op jit(solution)/shard_map/ppermute | solution.py:13
  88.5 11.4 %collective-permute-start.3 = (bf16[512,512]{1,0:T(8,128)(2,1)S(1)}, bf16[512,512]{1,0:T(8,128)(2,1)S(1)}, u32[]{:S(2)}, u32[]{:S(2)}) collective-permute-start(bf16[512,512]{1,0:T(8,128)(2,1)S(1)} %slice.9), channel_id=1, source_target_pairs={{3,0},{0,1},{1,2},{2,3},{7,4},{4,5},{5,6},{6,7},{11,8},{8,9},{9,10... | collective-permute-start | bytes 1572872 | tf_op jit(solution)/shard_map/ppermute | solution.py:13
  95.1 44.1 %collective-permute-start.15 = (bf16[1024,512]{1,0:T(8,128)(2,1)}, bf16[1024,512]{1,0:T(8,128)(2,1)S(1)}, u32[]{:S(2)}, u32[]{:S(2)}) collective-permute-start(bf16[1024,512]{1,0:T(8,128)(2,1)} %get-tuple-element.20), channel_id=1, source_target_pairs={{0,8},{8,0},{1,9},{9,1},{2,10},{10,2},{3,11},{11,3},{4,12},{12,4},... | collective-permute-start | bytes 3145736 | tf_op jit(solution)/shard_map/ppermute | solution.py:17
  101.3 4.3 %copy-start.3 = (bf16[1024,512]{1,0:T(8,128)(2,1)}, bf16[1024,512]{1,0:T(8,128)(2,1)S(1)}, u32[]{:S(2)}) copy-start(bf16[1024,512]{1,0:T(8,128)(2,1)S(1)} %convolution_convert_fusion.1) | copy-start | bytes 3145732
  105.5 33.7 %collective-permute-start.16 = (bf16[1024,512]{1,0:T(8,128)(2,1)}, bf16[1024,512]{1,0:T(8,128)(2,1)S(1)}, u32[]{:S(2)}, u32[]{:S(2)}) collective-permute-start(bf16[1024,512]{1,0:T(8,128)(2,1)} %get-tuple-element.22), channel_id=1, source_target_pairs={{0,8},{8,0},{1,9},{9,1},{2,10},{10,2},{3,11},{11,3},{4,12},{12,4},... | collective-permute-start | bytes 3145736 | tf_op jit(solution)/shard_map/ppermute | solution.py:17
  135.7 35.5 %collective-permute-start.6 = (bf16[1024,1024]{1,0:T(8,128)(2,1)}, bf16[1024,1024]{1,0:T(8,128)(2,1)}, u32[]{:S(2)}, u32[]{:S(2)}) collective-permute-start(bf16[1024,1024]{1,0:T(8,128)(2,1)} %bitcast), channel_id=1, source_target_pairs={{0,8},{8,0},{1,9},{9,1},{2,10},{10,2},{3,11},{11,3},{4,12},{12,4},... | collective-permute-start | bytes 6291464 | tf_op jit(solution)/shard_map/ppermute | solution.py:17
  144.6 25.2 %collective-permute-start.17 = (bf16[1024,512]{1,0:T(8,128)(2,1)}, bf16[1024,512]{1,0:T(8,128)(2,1)S(1)}, u32[]{:S(2)}, u32[]{:S(2)}) collective-permute-start(bf16[1024,512]{1,0:T(8,128)(2,1)} %get-tuple-element.6), channel_id=1, source_target_pairs={{0,128},{128,0},{1,129},{129,1},{2,130},{130,2},{3,131},{131,3},{4... | collective-permute-start | bytes 3145736 | tf_op jit(solution)/shard_map/ppermute | solution.py:17
  171.2 4.8 %copy-start.8 = (bf16[1024,512]{1,0:T(8,128)(2,1)S(1)}, bf16[1024,512]{1,0:T(8,128)(2,1)}, u32[]{:S(2)}) copy-start(bf16[1024,512]{1,0:T(8,128)(2,1)} %copy-done.7) | copy-start | bytes 3145732
  171.3 4.8 %copy-start.10 = (bf16[1024,512]{1,0:T(8,128)(2,1)S(1)}, bf16[1024,512]{1,0:T(8,128)(2,1)}, u32[]{:S(2)}) copy-start(bf16[1024,512]{1,0:T(8,128)(2,1)} %param.4) | copy-start | bytes 3145732
  182.3 25.8 %collective-permute-start.7 = (bf16[512,1024]{1,0:T(8,128)(2,1)S(1)}, bf16[512,1024]{1,0:T(8,128)(2,1)S(1)}, u32[]{:S(2)}, u32[]{:S(2)}) collective-permute-start(bf16[512,1024]{1,0:T(8,128)(2,1)S(1)} %fusion.17), channel_id=1, source_target_pairs={{0,4},{4,0},{1,5},{5,1},{2,6},{6,2},{3,7},{7,3},{8,12},{12,8},{9,1... | collective-permute-start | bytes 3145736 | tf_op jit(solution)/shard_map/ppermute | solution.py:17
  198.9 13.0 %collective-permute-start.18 = (bf16[128,512]{1,0:T(8,128)(2,1)}, bf16[128,512]{1,0:T(8,128)(2,1)S(1)}, u32[]{:S(2)}, u32[]{:S(2)}) collective-permute-start(bf16[128,512]{1,0:T(8,128)(2,1)} %reduce-scatter.2.cloned.1.call-done), channel_id=1, source_target_pairs={{0,0},{1,129},{2,10},{3,139},{8,1},{9,130},{10,11},{11,136},{128,2... | collective-permute-start | bytes 393224 | tf_op jit(solution)/shard_map/ppermute | solution.py:83
  210.8 5.3 %collective-permute-start.8 = (bf16[128,1024]{1,0:T(8,128)(2,1)S(1)}, bf16[128,1024]{1,0:T(8,128)(2,1)}, u32[]{:S(2)}, u32[]{:S(2)}) collective-permute-start(bf16[128,1024]{1,0:T(8,128)(2,1)S(1)} %get-tuple-element.13), channel_id=1, source_target_pairs={{1,0},{2,1},{3,2},{0,3},{5,4},{6,5},{7,6},{4,7},{9,8},{10,9},{11,1... | collective-permute-start | bytes 786440 | tf_op jit(solution)/shard_map/ppermute | solution.py:13
  212.9 8.2 %collective-permute-start.9 = (bf16[128,1024]{1,0:T(8,128)(2,1)}, bf16[128,1024]{1,0:T(8,128)(2,1)}, u32[]{:S(2)}, u32[]{:S(2)}) collective-permute-start(bf16[128,1024]{1,0:T(8,128)(2,1)} %get-tuple-element.12), channel_id=1, source_target_pairs={{2,0},{3,1},{0,2},{1,3},{6,4},{7,5},{4,6},{5,7},{10,8},{11,9},{8,1... | collective-permute-start | bytes 786440 | tf_op jit(solution)/shard_map/ppermute | solution.py:13
  214.4 14.0 %collective-permute-start.10 = (bf16[128,1024]{1,0:T(8,128)(2,1)S(1)}, bf16[128,1024]{1,0:T(8,128)(2,1)}, u32[]{:S(2)}, u32[]{:S(2)}) collective-permute-start(bf16[128,1024]{1,0:T(8,128)(2,1)S(1)} %get-tuple-element.11), channel_id=1, source_target_pairs={{3,0},{0,1},{1,2},{2,3},{7,4},{4,5},{5,6},{6,7},{11,8},{8,9},{9,10... | collective-permute-start | bytes 786440 | tf_op jit(solution)/shard_map/ppermute | solution.py:13
  (8 other events, 12.1 us)
Sparse Core Ops, SparseCore 0:
  171.4 27.5 reduce-scatter.1
